TPU v7x, 1024 devices: a whole 4x4x32 slice. The times are simulated.
1024 devices in a mesh: ctx: 128 (over z, x), tp: 8 (over y, core).
Axes of the slice: x: 4, y: 4, z: 32, core: 2. Of those that a mesh axis runs over, the one named last changes fastest.
Arguments:
- q_proj: bfloat16 [16384, 8192], P('ctx', 'tp'), may hold values from -110 to 110, as said below
- k_proj: bfloat16 [16384, 8192], P('ctx', 'tp'), may hold values from -6 to 6
- v_proj: bfloat16 [16384, 8192], P('ctx', 'tp'), may hold values from -6 to 6
- cotangent: bfloat16 [16384, 8192], P('ctx', 'tp'), may hold values from -6 to 6
- filters: float32 [128, 8192], P(None, 'tp'), may hold values from -0.5 to 0.5
- gain: float32 [8192], P('tp'), may hold values from 0.5 to 1.5
Outputs:
- grad_q: bfloat16 [16384, 8192], P('ctx', 'tp')
- grad_k: bfloat16 [16384, 8192], P('ctx', 'tp')
- grad_v: bfloat16 [16384, 8192], P('ctx', 'tp')
- grad_filters: float32 [128, 8192], P(None, 'tp')
- grad_gain: float32 [8192], P('tp')
Inputs may be any that keep to these rules, and one draw needn't show every extreme that they name: q_proj has entries of varying magnitude.
All inputs are finite; a program needn't handle non-finite values.
Results may differ from a plain program's by a relative error of at most 0.0049.
Values may be sent and summed in bfloat16 or wider, within the bound.
No kernel may reach another device: no remote copies, remote signals or barrier semaphores. Data moves between devices by JAX's collectives and lax.ppermute only.
A program may use at most 32 MiB of HBM per device.

v0:
```python
import jax
import jax.numpy as jnp
from jax import lax
from jax.experimental import pallas as pl
from jax.experimental.pallas import tpu as pltpu
from jax.sharding import Mesh, PartitionSpec as P

D = 8192
CTX = ("zh", "zl", "x")
NEAR = ("zl", "x")
FAR = "zh"
INWARDS = (4, 3, 5, 2, 6, 1, 7)
OUTWARDS = ((((0, 1),), ((0, 7),)), (((7, 5), (1, 2)),), (((7, 6), (2, 3), (5, 4)),))
EARLY = 1
LANES = 128
SUB = 8
VMEM_BYTES = 8 << 20


epsilon = 1e-06
f32 = jnp.float32
bf16 = jnp.bfloat16


def passed_along(value, by):
    length = lax.axis_size(CTX)
    pairs = [(i, i + by) for i in range(length) if 0 <= i + by < length]
    return lax.ppermute(value, CTX, pairs)


def shared(value, axes):
    size = lax.axis_size(axes)
    copies = jnp.broadcast_to(value[None], (size, *value.shape))
    return lax.all_to_all(copies, axes, 0, 0)


def far_sum(value):
    assert lax.axis_size(FAR) == 1 + len(INWARDS)
    parts = []
    for cube in INWARDS:
        parts.append(lax.ppermute(value, FAR, [(cube, 0)]))

    def total(extra):
        (*given, _) = lax.optimization_barrier((value, *parts, extra))
        whole = sum(part.astype(f32) for part in given).astype(bf16)
        whole = jnp.where(lax.axis_index(FAR) == 0, whole, jnp.zeros_like(whole))
        for steps in OUTWARDS:
            moved = []
            for pairs in steps:
                moved.append(lax.ppermute(whole, FAR, pairs))
            whole = sum(moved, whole)
        return whole

    return total


def call(kernel, outs, *operands, scratch=(), flops):
    in_vmem = pl.BlockSpec(memory_space=pltpu.VMEM)
    in_smem = pl.BlockSpec(memory_space=pltpu.SMEM)
    moved = sum(x.size * x.dtype.itemsize for x in (*operands, *outs))
    return pl.pallas_call(
        kernel,
        out_shape=outs,
        in_specs=[in_smem if x.dtype == jnp.int32 else in_vmem for x in operands],
        out_specs=tuple(in_vmem for _ in outs),
        scratch_shapes=list(scratch),
        compiler_params=pltpu.CompilerParams(vmem_limit_bytes=VMEM_BYTES),
        cost_estimate=pl.CostEstimate(flops=flops, bytes_accessed=moved, transcendentals=0),
    )(*operands)


def struct(shape, dtype):
    return jax.ShapeDtypeStruct(shape, dtype)


def over_tiles(width, body):
    def step(tile, carry):
        body(tile, pl.ds(pl.multiple_of(tile * LANES, LANES), LANES))
        return carry

    lax.fori_loop(0, width // LANES, step, 0)


def blocks(value):
    return [value[SUB * i : SUB * i + SUB] for i in range(value.shape[0] // SUB)]


def fill(window, at, value):
    window[pl.ds(at, value.shape[0]), :] = value.astype(f32)


def own_kernel(mixed, filters, conv, window):
    rows, width = mixed.shape
    count = rows // SUB
    window[pl.ds(0, SUB), :] = jnp.zeros((SUB, LANES), f32)

    def tile(_, lanes):
        fill(window, SUB, mixed[:, lanes])
        total = [None] * count
        for shift in range(SUB):
            slid = [window[pl.ds(SUB + SUB * i - shift, SUB), :] for i in range(count)]
            for step in range(count):
                weight = filters[pl.ds(SUB * step + shift, 1), lanes]
                for i in range(step, count):
                    term = weight * slid[i - step]
                    total[i] = term if total[i] is None else total[i] + term
        for i in range(count):
            conv[pl.ds(SUB * i, SUB), lanes] = total[i]

    over_tiles(width, tile)


def rim_kernel(own, earlier, filters, query, cot, gain, conv, sums, window, squares, crosses):
    rows, width = own.shape
    count = rows // SUB
    window[pl.ds(rows, SUB), :] = jnp.zeros((SUB, LANES), f32)
    squares[...] = jnp.zeros(squares.shape, f32)
    crosses[...] = jnp.zeros(crosses.shape, f32)

    def tile(_, lanes):
        fill(window, 0, earlier[:, lanes])
        total = [own[pl.ds(SUB * i, SUB), lanes] for i in range(count)]
        for shift in range(SUB):
            slid = [window[pl.ds(rows - SUB * i - shift, SUB), :] for i in range(count)]
            for step in range(count):
                weight = filters[pl.ds(SUB * step + shift, 1), lanes]
                for i in range(step + 1):
                    total[i] = total[i] + weight * slid[step - i]
        for i in range(count):
            at = pl.ds(SUB * i, SUB)
            conv[at, lanes] = total[i]
        whole = conv[:, lanes]
        product = query[:, lanes].astype(f32) * whole
        weighted = gain[:, lanes] * cot[:, lanes].astype(f32)
        squares[...] += product * product
        crosses[...] += weighted * product

    over_tiles(width, tile)
    square = jnp.sum(squares[...].T, 0, keepdims=True)
    cross = jnp.sum(crosses[...].T, 0, keepdims=True)
    first = lax.broadcasted_iota(jnp.int32, sums.shape[1:], 0) == 0
    both = jnp.where(first, square, cross)
    for i in range(sums.shape[0]):
        sums[i] = both


def gathered(parts):
    row = lax.broadcasted_iota(jnp.int32, (SUB, LANES), 0)
    half = 1
    while half < SUB:
        low = (row & half) == 0
        parts = [
            jnp.where(low, a, b) + pltpu.roll(jnp.where(low, b, a), half, 0)
            for a, b in zip(parts[::2], parts[1::2])
        ]
        half *= 2
    return parts[0]


def grads_kernel(
    sums, conv, query, cot, gain, earlier, mixed, grad_conv, grad_q, block, window, inverse, pull, partial
):
    rows, width = conv.shape
    count = rows // SUB
    both = jnp.sum(sums[...], 0)
    rms = jnp.sqrt(both[0:1] / D + epsilon)
    inverse[...] = jnp.broadcast_to(1.0 / rms, (LANES, rows)).T
    pull[...] = jnp.broadcast_to(both[1:2] / (D * (rms * rms * rms)), (LANES, rows)).T
    block[:, width:] = jnp.zeros((rows, LANES), bf16)

    def tile(index, lanes):
        whole = conv[:, lanes]
        query_f32 = query[:, lanes].astype(f32)
        cot_f32 = cot[:, lanes].astype(f32)
        product = query_f32 * whole
        grad_product = gain[:, lanes] * cot_f32 * inverse[...] - product * pull[...]
        rounded = (query_f32 * grad_product).astype(bf16)
        grad_conv[:, lanes] = rounded
        grad_q[:, lanes] = (grad_product * whole).astype(bf16)
        gains = jnp.sum((cot_f32 * product * inverse[...]).reshape(count, SUB, LANES), 0)
        block[pl.ds(pl.multiple_of(index * SUB, SUB), SUB), width:] = gains.astype(bf16)
        fill(window, 0, earlier[:, lanes])
        fill(window, rows, mixed[:, lanes])
        ours = blocks(rounded.astype(f32))
        for shift in range(SUB):
            slid = [window[pl.ds(SUB * (i + 1) - shift, SUB), :] for i in range(2 * count - 1)]
            for step in range(count):
                terms = [ours[i] * slid[count - 1 + i - step] for i in range(count)]
                while len(terms) > 1:
                    terms = [a + b for a, b in zip(terms[::2], terms[1::2])]
                partial[SUB * step + shift] = terms[0]
        for step in range(0, count, 2):
            pair = [gathered([partial[SUB * s + i] for i in range(SUB)]) for s in (step, step + 1)]
            block[pl.ds(SUB * step, 2 * SUB), lanes] = jnp.concatenate(pair, 0).astype(bf16)

    over_tiles(width, tile)


def back(grad_conv, later, filters, k_proj, v_proj, grad_k, grad_v, window):
    rows, width = grad_conv.shape
    count = rows // SUB

    def tile(_, lanes):
        fill(window, 0, grad_conv[:, lanes])
        fill(window, rows, later[:, lanes])
        total = [jnp.zeros((SUB, LANES), f32)] * count
        for shift in range(SUB):
            slid = [window[pl.ds(SUB * i + shift, SUB), :] for i in range(2 * count - 1)]
            for step in range(count):
                weight = filters[pl.ds(SUB * step + shift, 1), lanes]
                for i in range(count):
                    total[i] = total[i] + weight * slid[i + step]
        grad_mixed = jnp.concatenate(total, 0)
        grad_k[:, lanes] = (grad_mixed * v_proj[:, lanes].astype(f32)).astype(bf16)
        grad_v[:, lanes] = (grad_mixed * k_proj[:, lanes].astype(f32)).astype(bf16)

    over_tiles(width, tile)


def early_back_kernel(early, *refs):
    @pl.when(early[0] == 1)
    def _():
        back(*refs)


def late_back_kernel(early, early_k, early_v, *refs):
    grad_k, grad_v = refs[-3:-1]

    @pl.when(early[0] == 1)
    def _():
        grad_k[...] = early_k[...]
        grad_v[...] = early_v[...]

    @pl.when(early[0] == 0)
    def _():
        back(*refs)


def final_kernel(whole, grad_filters, grad_gain):
    width = grad_filters.shape[1]
    grad_filters[...] = whole[:, :width].astype(f32)
    for i in range(width // LANES):
        part = whole[pl.ds(SUB * i, SUB), width:].astype(f32)
        grad_gain[pl.ds(i, 1), :] = jnp.sum(part, 0, keepdims=True)


def device_part(q_proj, k_proj, v_proj, cotangent, filters, gain):
    rows, width = q_proj.shape
    macs = 2 * filters.shape[0] * rows * width
    tile = pltpu.VMEM((rows, LANES), f32)
    short = pltpu.VMEM((rows + SUB, LANES), f32)
    long = pltpu.VMEM((2 * rows, LANES), f32)
    gain = gain.reshape(1, width)
    mixed = (k_proj.astype(f32) * v_proj.astype(f32)).astype(bf16)
    earlier = passed_along(mixed, 1)
    (own,) = call(own_kernel, (struct((rows, width), f32),), mixed, filters, scratch=(short,), flops=macs // 2)
    members = lax.axis_size("tp")
    conv, sums = call(
        rim_kernel,
        (struct((rows, width), f32), struct((members, SUB, rows), f32)),
        own,
        earlier,
        filters,
        q_proj,
        cotangent,
        gain,
        scratch=(short, tile, tile),
        flops=macs // 2,
    )
    sums = lax.all_to_all(sums, "tp", 0, 0)
    grad_conv, grad_q, block = call(
        grads_kernel,
        (struct((rows, width), bf16), struct((rows, width), bf16), struct((rows, width + LANES), bf16)),
        sums,
        conv,
        q_proj,
        cotangent,
        gain,
        earlier,
        mixed,
        scratch=(long, tile, tile, pltpu.VMEM((rows, SUB, LANES), f32)),
        flops=macs,
    )
    near = lax.axis_size(NEAR)
    block = block.reshape(near, rows // near, width + LANES)
    block = lax.all_to_all(block, NEAR, 0, 0)
    block = jnp.sum(block.astype(f32), 0).astype(bf16)
    block, grad_conv = lax.optimization_barrier((block, grad_conv))
    total = far_sum(block)
    later = passed_along(grad_conv, -1)
    early = (lax.axis_index(FAR) < EARLY).astype(jnp.int32).reshape(1)
    grads = (struct((rows, width), bf16), struct((rows, width), bf16))
    sources = (grad_conv, later, filters, k_proj, v_proj)
    early_k, early_v = call(early_back_kernel, grads, early, *sources, scratch=(long,), flops=macs)
    whole = total(early_k)
    grad_k, grad_v = call(late_back_kernel, grads, early, early_k, early_v, *sources, scratch=(long,), flops=macs)
    whole, grad_k = lax.optimization_barrier((whole, grad_k))
    whole = shared(whole, NEAR).reshape(rows, width + LANES)
    grad_filters, grad_gain = call(
        final_kernel, (struct((rows, width), f32), struct((width // LANES, LANES), f32)), whole, flops=0
    )
    return (grad_q, grad_k, grad_v, grad_filters, grad_gain.reshape(width))


def solution(mesh):
    cube = 4
    far = mesh.devices.shape[0] // (cube * cube)
    split = Mesh(mesh.devices.reshape(far, cube, cube, -1), (*CTX, "tp"))
    rows = P(CTX, "tp")
    in_specs = (rows, rows, rows, rows, P(None, "tp"), P("tp"))
    out_specs = (rows, rows, rows, P(None, "tp"), P("tp"))
    return jax.shard_map(device_part, mesh=split, in_specs=in_specs, out_specs=out_specs, check_vma=False)
```

profile of v0, /device:TPU:128, one launch (start us, length us, event | category | flops | bytes accessed | tf_op | source)
XLA Modules:
  0.0 123.1 jit_solution(2780875360039918357)
XLA Ops:
  0.6 1.2 multiply_convert_fusion.mixed
  1.8 3.5 %collective-permute-start = (bf16[128,1024]{1,0:T(8,128)(2,1)S(1)}, bf16[128,1024]{1,0:T(8,128)(2,1)S(1)}, u32[]{:S(2)}, u32[]{:S(2)}) collective-permute-start(bf16[128,1024]{1,0:T(8,128)(2,1)S(1)} %multiply_convert_fusion.mixed), channel_id=1, source_target_pairs={{0,8},{8,16},{16,24},{24,32},{32,40},{40,48},{48,56},{56,64},{64,7... | collective-permute-start | bytes 786440 | tf_op jit(solution)/shard_map/ppermute | solution.py:28
  5.4 2.4 %shard_map.101.own = f32[128,1024]{1,0:T(8,128)S(1)} custom-call(bf16[128,1024]{1,0:T(8,128)(2,1)S(1)} %multiply_convert_fusion.mixed, f32[128,1024]{1,0:T(8,128)S(1)} %copy-done), custom_call_target="tpu_custom_call" | custom-call | flops 16777216 | bytes 1310720 | tf_op jit(solution)/shard_map/pallas_call | solution.py:61
  7.8 7.4 %collective-permute-done.earlier = bf16[128,1024]{1,0:T(8,128)(2,1)S(1)} collective-permute-done((bf16[128,1024]{1,0:T(8,128)(2,1)S(1)}, bf16[128,1024]{1,0:T(8,128)(2,1)S(1)}, u32[]{:S(2)}, u32[]{:S(2)}) %collective-permute-start) | collective-permute-done | bytes 262176 | tf_op jit(solution)/shard_map/ppermute | solution.py:28
  15.2 2.8 %shard_map.102 = (f32[128,1024]{1,0:T(8,128)S(1)}, f32[8,8,128]{2,1,0:T(8,128)S(1)}) custom-call(f32[128,1024]{1,0:T(8,128)S(1)} %shard_map.101.own, bf16[128,1024]{1,0:T(8,128)(2,1)S(1)} %collective-permute-done.earlier, f32[128,1024]{1,0:T(8,128)S(1)} %copy-done, bf16[128,1024]{1,0:T(8,128)(2,1)S(1)} %copy-done.3, bf16[128,1024]{1,0:T(8,128)(2,1)S(1)} %copy-done.4, ...), custom_call_target="tpu_custom_call" | custom-call | flops 16777216 | bytes 2396160 | tf_op jit(solution)/shard_map/pallas_call | solution.py:61
  18.0 9.7 %all_to_all.15.sums = f32[8,8,128]{2,1,0:T(8,128)S(1)} all-to-all(f32[8,8,128]{2,1,0:T(8,128)S(1)} %get-tuple-element.28), channel_id=1, replica_groups=mesh['zh'=8,'zl'=4,'x'=4,'tp'=8] {'tp'}, dimensions={0} | all-to-all | bytes 65536 | tf_op jit(solution)/shard_map/all_to_all | solution.py:270
  27.7 5.7 %shard_map.103 = (bf16[128,1024]{1,0:T(8,128)(2,1)S(1)}, bf16[128,1024]{1,0:T(8,128)(2,1)}, bf16[128,1152]{1,0:T(8,128)(2,1)S(1)}) custom-call(f32[8,8,128]{2,1,0:T(8,128)S(1)} %all_to_all.15.sums, f32[128,1024]{1,0:T(8,128)S(1)} %get-tuple-element.29.conv, bf16[128,1024]{1,0:T(8,128)(2,1)S(1)} %copy-done.3, bf16[128,1024]{1,0:T(8,128)(2,1)S(1)} %copy-done.4, ...), custom_call_target="tpu_custom_call" | custom-call | flops 33554432 | bytes 2428928 | tf_op jit(solution)/shard_map/pallas_call | solution.py:61
  33.4 16.5 %all_to_all.16 = bf16[16,8,1152]{2,1,0:T(8,128)(2,1)S(1)} all-to-all(bf16[16,8,1152]{2,1,0:T(8,128)(2,1)S(1)} %bitcast.6), channel_id=1, replica_groups=mesh['zh'=8,'zl'=4,'x'=4,'tp'=8] {'zl','x'}, dimensions={0} | all-to-all | bytes 589824 | tf_op jit(solution)/shard_map/all_to_all | solution.py:286
  49.9 2.1 %collective-permute-start.8 = (bf16[128,1024]{1,0:T(8,128)(2,1)S(1)}, bf16[128,1024]{1,0:T(8,128)(2,1)S(1)}, u32[]{:S(2)}, u32[]{:S(2)}) collective-permute-start(bf16[128,1024]{1,0:T(8,128)(2,1)S(1)} %get-tuple-element.34.refs_0_), channel_id=1, source_target_pairs={{8,0},{16,8},{24,16},{32,24},{40,32},{48,40},{56,48},{64,56},{72,6... | collective-permute-start | bytes 786440 | tf_op jit(solution)/shard_map/ppermute | solution.py:28
  52.0 0.7 collective-permute-start.1
  53.3 0.7 collective-permute-start.3
  54.0 0.7 collective-permute-start.4
  54.7 0.7 collective-permute-start.5
  55.4 26.3 %collective-permute-start.6 = (bf16[8,1152]{1,0:T(8,128)(2,1)S(1)}, bf16[8,1152]{1,0:T(8,128)(2,1)S(1)}, u32[]{:S(2)}, u32[]{:S(2)}) collective-permute-start(bf16[8,1152]{1,0:T(8,128)(2,1)S(1)} %reduce_sum.12), channel_id=1, source_target_pairs={{128,0},{129,1},{130,2},{131,3},{132,4},{133,5},{134,6},{135,7},{1... | collective-permute-start | bytes 55304 | tf_op jit(solution)/shard_map/ppermute | solution.py:41
  81.7 0.7 collective-permute-start.7
  82.5 0.7 collective-permute-done.6
  83.2 0.7 collective-permute-start.10
  83.8 1.3 %collective-permute-start.9 = (bf16[8,1152]{1,0:T(8,128)(2,1)S(1)}, bf16[8,1152]{1,0:T(8,128)(2,1)S(1)}, u32[]{:S(2)}, u32[]{:S(2)}) collective-permute-start(bf16[8,1152]{1,0:T(8,128)(2,1)S(1)} %fusion), channel_id=1, source_target_pairs={{0,128},{1,129},{2,130},{3,131},{4,132},{5,133},{6,134},{7,135},{8... | collective-permute-start | bytes 55304 | tf_op jit(solution)/shard_map/ppermute | solution.py:50
  85.2 12.0 %collective-permute-done.9 = bf16[8,1152]{1,0:T(8,128)(2,1)S(1)} collective-permute-done((bf16[8,1152]{1,0:T(8,128)(2,1)S(1)}, bf16[8,1152]{1,0:T(8,128)(2,1)S(1)}, u32[]{:S(2)}, u32[]{:S(2)}) %collective-permute-start.9) | collective-permute-done | bytes 18464 | tf_op jit(solution)/shard_map/ppermute | solution.py:50
  97.2 1.3 %collective-permute-start.11 = (bf16[8,1152]{1,0:T(8,128)(2,1)S(1)}, bf16[8,1152]{1,0:T(8,128)(2,1)S(1)}, u32[]{:S(2)}, u32[]{:S(2)}) collective-permute-start(bf16[8,1152]{1,0:T(8,128)(2,1)S(1)} %add_add_fusion), channel_id=1, source_target_pairs={{896,640},{128,256},{897,641},{129,257},{898,642},{130,258},{899,6... | collective-permute-start | bytes 55304 | tf_op jit(solution)/shard_map/ppermute | solution.py:50
  98.5 1.4 %collective-permute-done.11 = bf16[8,1152]{1,0:T(8,128)(2,1)S(1)} collective-permute-done((bf16[8,1152]{1,0:T(8,128)(2,1)S(1)}, bf16[8,1152]{1,0:T(8,128)(2,1)S(1)}, u32[]{:S(2)}, u32[]{:S(2)}) %collective-permute-start.11) | collective-permute-done | bytes 18464 | tf_op jit(solution)/shard_map/ppermute | solution.py:50
  100.6 5.4 %shard_map.105 = (bf16[128,1024]{1,0:T(8,128)(2,1)}, bf16[128,1024]{1,0:T(8,128)(2,1)}) custom-call(s32[1]{0:T(128)} %bitcast.2.early, bf16[128,1024]{1,0:T(8,128)(2,1)S(1)} %get-tuple-element.35.early_k, bf16[128,1024]{1,0:T(8,128)(2,1)S(1)} %get-tuple-element.44.early_v, bf16[128,1024]{1,0:T(8,128)(2,1)S(1)} %get-tuple-element.34.refs_0_, ...), custom_call_target="tpu_custom_call" | custom-call | flops 33554432 | bytes 2621444 | tf_op jit(solution)/shard_map/pallas_call | solution.py:61
  106.1 16.1 %all_to_all.17 = bf16[16,8,1152]{2,1,0:T(8,128)(2,1)S(1)} all-to-all(bf16[16,8,1152]{2,1,0:T(8,128)(2,1)S(1)} %broadcast_in_dim.10), channel_id=1, replica_groups=mesh['zh'=8,'zl'=4,'x'=4,'tp'=8] {'zl','x'}, dimensions={0} | all-to-all | bytes 589824 | tf_op jit(solution)/shard_map/all_to_all | solution.py:34
  122.3 0.8 shard_map.106
  (30 shorter events, 1.5 us)
Async XLA Ops:
  0.6 4.7 %copy-start = (f32[128,1024]{1,0:T(8,128)S(1)}, f32[128,1024]{1,0:T(8,128)}, u32[]{:S(2)}) copy-start(f32[128,1024]{1,0:T(8,128)} %refs_2_.3) | copy-start | bytes 1572868
  1.8 13.4 %copy-start.3 = (bf16[128,1024]{1,0:T(8,128)(2,1)S(1)}, bf16[128,1024]{1,0:T(8,128)(2,1)}, u32[]{:S(2)}) copy-start(bf16[128,1024]{1,0:T(8,128)(2,1)} %query.3) | copy-start | bytes 786436
  1.8 13.4 %copy-start.4 = (bf16[128,1024]{1,0:T(8,128)(2,1)S(1)}, bf16[128,1024]{1,0:T(8,128)(2,1)}, u32[]{:S(2)}) copy-start(bf16[128,1024]{1,0:T(8,128)(2,1)} %cot.3) | copy-start | bytes 786436
  1.8 13.4 %collective-permute-start = (bf16[128,1024]{1,0:T(8,128)(2,1)S(1)}, bf16[128,1024]{1,0:T(8,128)(2,1)S(1)}, u32[]{:S(2)}, u32[]{:S(2)}) collective-permute-start(bf16[128,1024]{1,0:T(8,128)(2,1)S(1)} %multiply_convert_fusion.mixed), channel_id=1, source_target_pairs={{0,8},{8,16},{16,24},{24,32},{32,40},{40,48},{48,56},{56,64},{64,7... | collective-permute-start | bytes 786440 | tf_op jit(solution)/shard_map/ppermute | solution.py:28
  5.4 9.8 %copy-start.5 = (f32[1024]{0:T(1024)S(1)}, f32[1024]{0:T(1024)}, u32[]{:S(2)}) copy-start(f32[1024]{0:T(1024)} %param.11) | copy-start | bytes 12292
  33.4 49.0 %copy-start.2 = (bf16[128,1024]{1,0:T(8,128)(2,1)S(1)}, bf16[128,1024]{1,0:T(8,128)(2,1)}, u32[]{:S(2)}) copy-start(bf16[128,1024]{1,0:T(8,128)(2,1)} %refs_3_.3) | copy-start | bytes 786436
  49.9 32.5 %copy-start.1 = (bf16[128,1024]{1,0:T(8,128)(2,1)S(1)}, bf16[128,1024]{1,0:T(8,128)(2,1)}, u32[]{:S(2)}) copy-start(bf16[128,1024]{1,0:T(8,128)(2,1)} %refs_4_.3) | copy-start | bytes 786436
  49.9 31.8 %collective-permute-start.8 = (bf16[128,1024]{1,0:T(8,128)(2,1)S(1)}, bf16[128,1024]{1,0:T(8,128)(2,1)S(1)}, u32[]{:S(2)}, u32[]{:S(2)}) collective-permute-start(bf16[128,1024]{1,0:T(8,128)(2,1)S(1)} %get-tuple-element.34.refs_0_), channel_id=1, source_target_pairs={{8,0},{16,8},{24,16},{32,24},{40,32},{48,40},{56,48},{64,56},{72,6... | collective-permute-start | bytes 786440 | tf_op jit(solution)/shard_map/ppermute | solution.py:28
  52.0 2.7 %collective-permute-start.1 = (bf16[8,1152]{1,0:T(8,128)(2,1)S(1)}, bf16[8,1152]{1,0:T(8,128)(2,1)S(1)}, u32[]{:S(2)}, u32[]{:S(2)}) collective-permute-start(bf16[8,1152]{1,0:T(8,128)(2,1)S(1)} %reduce_sum.12), channel_id=1, source_target_pairs={{512,0},{513,1},{514,2},{515,3},{516,4},{517,5},{518,6},{519,7},{5... | collective-permute-start | bytes 55304 | tf_op jit(solution)/shard_map/ppermute | solution.py:41
  52.6 2.7 %collective-permute-start.2 = (bf16[8,1152]{1,0:T(8,128)(2,1)S(1)}, bf16[8,1152]{1,0:T(8,128)(2,1)S(1)}, u32[]{:S(2)}, u32[]{:S(2)}) collective-permute-start(bf16[8,1152]{1,0:T(8,128)(2,1)S(1)} %reduce_sum.12), channel_id=1, source_target_pairs={{384,0},{385,1},{386,2},{387,3},{388,4},{389,5},{390,6},{391,7},{3... | collective-permute-start | bytes 55304 | tf_op jit(solution)/shard_map/ppermute | solution.py:41
  53.3 29.1 %collective-permute-start.3 = (bf16[8,1152]{1,0:T(8,128)(2,1)S(1)}, bf16[8,1152]{1,0:T(8,128)(2,1)S(1)}, u32[]{:S(2)}, u32[]{:S(2)}) collective-permute-start(bf16[8,1152]{1,0:T(8,128)(2,1)S(1)} %reduce_sum.12), channel_id=1, source_target_pairs={{640,0},{641,1},{642,2},{643,3},{644,4},{645,5},{646,6},{647,7},{6... | collective-permute-start | bytes 55304 | tf_op jit(solution)/shard_map/ppermute | solution.py:41
  54.0 28.4 %collective-permute-start.4 = (bf16[8,1152]{1,0:T(8,128)(2,1)S(1)}, bf16[8,1152]{1,0:T(8,128)(2,1)S(1)}, u32[]{:S(2)}, u32[]{:S(2)}) collective-permute-start(bf16[8,1152]{1,0:T(8,128)(2,1)S(1)} %reduce_sum.12), channel_id=1, source_target_pairs={{256,0},{257,1},{258,2},{259,3},{260,4},{261,5},{262,6},{263,7},{2... | collective-permute-start | bytes 55304 | tf_op jit(solution)/shard_map/ppermute | solution.py:41
  54.7 27.8 %collective-permute-start.5 = (bf16[8,1152]{1,0:T(8,128)(2,1)S(1)}, bf16[8,1152]{1,0:T(8,128)(2,1)S(1)}, u32[]{:S(2)}, u32[]{:S(2)}) collective-permute-start(bf16[8,1152]{1,0:T(8,128)(2,1)S(1)} %reduce_sum.12), channel_id=1, source_target_pairs={{768,0},{769,1},{770,2},{771,3},{772,4},{773,5},{774,6},{775,7},{7... | collective-permute-start | bytes 55304 | tf_op jit(solution)/shard_map/ppermute | solution.py:41
  55.4 27.8 %collective-permute-start.6 = (bf16[8,1152]{1,0:T(8,128)(2,1)S(1)}, bf16[8,1152]{1,0:T(8,128)(2,1)S(1)}, u32[]{:S(2)}, u32[]{:S(2)}) collective-permute-start(bf16[8,1152]{1,0:T(8,128)(2,1)S(1)} %reduce_sum.12), channel_id=1, source_target_pairs={{128,0},{129,1},{130,2},{131,3},{132,4},{133,5},{134,6},{135,7},{1... | collective-permute-start | bytes 55304 | tf_op jit(solution)/shard_map/ppermute | solution.py:41
  81.7 1.4 %collective-permute-start.7 = (bf16[8,1152]{1,0:T(8,128)(2,1)S(1)}, bf16[8,1152]{1,0:T(8,128)(2,1)S(1)}, u32[]{:S(2)}, u32[]{:S(2)}) collective-permute-start(bf16[8,1152]{1,0:T(8,128)(2,1)S(1)} %reduce_sum.12), channel_id=1, source_target_pairs={{896,0},{897,1},{898,2},{899,3},{900,4},{901,5},{902,6},{903,7},{9... | collective-permute-start | bytes 55304 | tf_op jit(solution)/shard_map/ppermute | solution.py:41
  83.2 2.0 %collective-permute-start.10 = (bf16[8,1152]{1,0:T(8,128)(2,1)S(1)}, bf16[8,1152]{1,0:T(8,128)(2,1)S(1)}, u32[]{:S(2)}, u32[]{:S(2)}) collective-permute-start(bf16[8,1152]{1,0:T(8,128)(2,1)S(1)} %fusion), channel_id=1, source_target_pairs={{0,896},{1,897},{2,898},{3,899},{4,900},{5,901},{6,902},{7,903},{8... | collective-permute-start | bytes 55304 | tf_op jit(solution)/shard_map/ppermute | solution.py:50
  83.8 13.3 %collective-permute-start.9 = (bf16[8,1152]{1,0:T(8,128)(2,1)S(1)}, bf16[8,1152]{1,0:T(8,128)(2,1)S(1)}, u32[]{:S(2)}, u32[]{:S(2)}) collective-permute-start(bf16[8,1152]{1,0:T(8,128)(2,1)S(1)} %fusion), channel_id=1, source_target_pairs={{0,128},{1,129},{2,130},{3,131},{4,132},{5,133},{6,134},{7,135},{8... | collective-permute-start | bytes 55304 | tf_op jit(solution)/shard_map/ppermute | solution.py:50
  97.2 2.7 %collective-permute-start.11 = (bf16[8,1152]{1,0:T(8,128)(2,1)S(1)}, bf16[8,1152]{1,0:T(8,128)(2,1)S(1)}, u32[]{:S(2)}, u32[]{:S(2)}) collective-permute-start(bf16[8,1152]{1,0:T(8,128)(2,1)S(1)} %add_add_fusion), channel_id=1, source_target_pairs={{896,640},{128,256},{897,641},{129,257},{898,642},{130,258},{899,6... | collective-permute-start | bytes 55304 | tf_op jit(solution)/shard_map/ppermute | solution.py:50
  99.9 6.1 %collective-permute-start.12 = (bf16[8,1152]{1,0:T(8,128)(2,1)S(1)}, bf16[8,1152]{1,0:T(8,128)(2,1)S(1)}, u32[]{:S(2)}, u32[]{:S(2)}) collective-permute-start(bf16[8,1152]{1,0:T(8,128)(2,1)S(1)} %add.42), channel_id=1, source_target_pairs={{896,768},{256,384},{640,512},{897,769},{257,385},{641,513},{898,7... | collective-permute-start | bytes 55304 | tf_op jit(solution)/shard_map/ppermute | solution.py:50
where the time goes:
time: 124 us; the launch traced here: 123 us
  blocking collectives  42.4 us (34%)
  starting transfers between devices  39.8 us (32%)
  waiting for transfers between devices  21.6 us (17%)
  Pallas kernels  17.1 us (14%)
  other arithmetic  1.25 us (1%)
    ppermute x7, starting transfers between devices, far_sum(): parts.append(lax.ppermute(value, FAR, [(cube, 0)]))  30.3 us
    pallas_call x6, Pallas kernels, call(): pl.pallas_call(kernel, out_shape=outs, in_specs=[in_smem if x.dtype == jn...  17.1 us
    all_to_all x1, blocking collectives, device_part(): block = lax.all_to_all(block, NEAR, 0, 0)  16.5 us
    all_to_all x1, blocking collectives, shared(): return lax.all_to_all(copies, axes, 0, 0)  16.1 us
    ppermute x4, waiting for transfers between devices, total(): moved.append(lax.ppermute(whole, FAR, pairs))  13.5 us
    all_to_all x1, blocking collectives, device_part(): sums = lax.all_to_all(sums, 'tp', 0, 0)  9.72 us
    ppermute x2, waiting for transfers between devices, passed_along(): return lax.ppermute(value, CTX, pairs)  7.43 us
    ppermute x2, starting transfers between devices, passed_along(): return lax.ppermute(value, CTX, pairs)  5.58 us
  transfers between devices with their start and end apart: 13, of which 4 were waited for; matrix products, arithmetic and copies ran while one was open for 0% of the time, Pallas kernels for 6%

commit v1 on v0

--- a/solution.py
+++ b/solution.py
@@ -9,8 +9,12 @@
 CTX = ("zh", "zl", "x")
 NEAR = ("zl", "x")
 FAR = "zh"
-INWARDS = (4, 3, 5, 2, 6, 1, 7)
-OUTWARDS = ((((0, 1),), ((0, 7),)), (((7, 5), (1, 2)),), (((7, 6), (2, 3), (5, 4)),))
+INWARDS = (4, 5, 3, 2, 6, 1, 7)
+OUTWARDS = (
+    (((0, 1),), ((0, 7),)),
+    (((7, 4), (1, 2)), ((7, 5),)),
+    (((7, 6), (2, 3)),),
+)
 EARLY = 1
 LANES = 128
 SUB = 8

time: 124 us -> 124 us (level)
    ppermute x4 -> x5, waiting for transfers between devices: 13.5 us -> 12.8 us  [total(): moved.append(lax.ppermute(whole, FAR, pairs))]
    ppermute x4 -> x5, starting transfers between devices: 3.9 us -> 4.56 us  [total(): moved.append(lax.ppermute(whole, FAR, pairs))]
  transfers between devices with their start and end apart: 13 -> 14, of which waited for: 4 -> 4; matrix products, arithmetic and copies ran while one was open for 0% -> 0% of each run, Pallas kernels for 6% -> 6%
where the time goes in v1:
time: 124 us; the launch traced here: 123 us
  blocking collectives  42.4 us (34%)
  starting transfers between devices  40.5 us (33%)
  waiting for transfers between devices  21 us (17%)
  Pallas kernels  17.1 us (14%)
  other arithmetic  1.25 us (1%)
    ppermute x7, starting transfers between devices, far_sum(): parts.append(lax.ppermute(value, FAR, [(cube, 0)]))  30.3 us
    pallas_call x6, Pallas kernels, call(): pl.pallas_call(kernel, out_shape=outs, in_specs=[in_smem if x.dtype == jn...  17.1 us
    all_to_all x1, blocking collectives, device_part(): block = lax.all_to_all(block, NEAR, 0, 0)  16.5 us
    all_to_all x1, blocking collectives, shared(): return lax.all_to_all(copies, axes, 0, 0)  16.1 us
    ppermute x5, waiting for transfers between devices, total(): moved.append(lax.ppermute(whole, FAR, pairs))  12.8 us
    all_to_all x1, blocking collectives, device_part(): sums = lax.all_to_all(sums, 'tp', 0, 0)  9.72 us
    ppermute x2, waiting for transfers between devices, passed_along(): return lax.ppermute(value, CTX, pairs)  7.43 us
    ppermute x2, starting transfers between devices, passed_along(): return lax.ppermute(value, CTX, pairs)  5.58 us
  transfers between devices with their start and end apart: 14, of which 4 were waited for; matrix products, arithmetic and copies ran while one was open for 0% of the time, Pallas kernels for 6%

profile of v1, /device:TPU:128, one launch (start us, length us, event | category | flops | bytes accessed | tf_op | source)
XLA Modules:
  0.0 123.1 jit_solution(10505980491158467802)
XLA Ops:
  0.6 1.2 multiply_convert_fusion.mixed
  1.8 3.5 %collective-permute-start = (bf16[128,1024]{1,0:T(8,128)(2,1)S(1)}, bf16[128,1024]{1,0:T(8,128)(2,1)S(1)}, u32[]{:S(2)}, u32[]{:S(2)}) collective-permute-start(bf16[128,1024]{1,0:T(8,128)(2,1)S(1)} %multiply_convert_fusion.mixed), channel_id=1, source_target_pairs={{0,8},{8,16},{16,24},{24,32},{32,40},{40,48},{48,56},{56,64},{64,7... | collective-permute-start | bytes 786440 | tf_op jit(solution)/shard_map/ppermute | solution.py:32
  5.4 2.4 %shard_map.101.own = f32[128,1024]{1,0:T(8,128)S(1)} custom-call(bf16[128,1024]{1,0:T(8,128)(2,1)S(1)} %multiply_convert_fusion.mixed, f32[128,1024]{1,0:T(8,128)S(1)} %copy-done), custom_call_target="tpu_custom_call" | custom-call | flops 16777216 | bytes 1310720 | tf_op jit(solution)/shard_map/pallas_call | solution.py:65
  7.8 7.4 %collective-permute-done.earlier = bf16[128,1024]{1,0:T(8,128)(2,1)S(1)} collective-permute-done((bf16[128,1024]{1,0:T(8,128)(2,1)S(1)}, bf16[128,1024]{1,0:T(8,128)(2,1)S(1)}, u32[]{:S(2)}, u32[]{:S(2)}) %collective-permute-start) | collective-permute-done | bytes 262176 | tf_op jit(solution)/shard_map/ppermute | solution.py:32
  15.2 2.8 %shard_map.102 = (f32[128,1024]{1,0:T(8,128)S(1)}, f32[8,8,128]{2,1,0:T(8,128)S(1)}) custom-call(f32[128,1024]{1,0:T(8,128)S(1)} %shard_map.101.own, bf16[128,1024]{1,0:T(8,128)(2,1)S(1)} %collective-permute-done.earlier, f32[128,1024]{1,0:T(8,128)S(1)} %copy-done, bf16[128,1024]{1,0:T(8,128)(2,1)S(1)} %copy-done.3, bf16[128,1024]{1,0:T(8,128)(2,1)S(1)} %copy-done.4, ...), custom_call_target="tpu_custom_call" | custom-call | flops 16777216 | bytes 2396160 | tf_op jit(solution)/shard_map/pallas_call | solution.py:65
  18.0 9.7 %all_to_all.15.sums = f32[8,8,128]{2,1,0:T(8,128)S(1)} all-to-all(f32[8,8,128]{2,1,0:T(8,128)S(1)} %get-tuple-element.28), channel_id=1, replica_groups=mesh['zh'=8,'zl'=4,'x'=4,'tp'=8] {'tp'}, dimensions={0} | all-to-all | bytes 65536 | tf_op jit(solution)/shard_map/all_to_all | solution.py:274
  27.7 5.7 %shard_map.103 = (bf16[128,1024]{1,0:T(8,128)(2,1)S(1)}, bf16[128,1024]{1,0:T(8,128)(2,1)}, bf16[128,1152]{1,0:T(8,128)(2,1)S(1)}) custom-call(f32[8,8,128]{2,1,0:T(8,128)S(1)} %all_to_all.15.sums, f32[128,1024]{1,0:T(8,128)S(1)} %get-tuple-element.29.conv, bf16[128,1024]{1,0:T(8,128)(2,1)S(1)} %copy-done.3, bf16[128,1024]{1,0:T(8,128)(2,1)S(1)} %copy-done.4, ...), custom_call_target="tpu_custom_call" | custom-call | flops 33554432 | bytes 2428928 | tf_op jit(solution)/shard_map/pallas_call | solution.py:65
  33.4 16.5 %all_to_all.16 = bf16[16,8,1152]{2,1,0:T(8,128)(2,1)S(1)} all-to-all(bf16[16,8,1152]{2,1,0:T(8,128)(2,1)S(1)} %bitcast.6), channel_id=1, replica_groups=mesh['zh'=8,'zl'=4,'x'=4,'tp'=8] {'zl','x'}, dimensions={0} | all-to-all | bytes 589824 | tf_op jit(solution)/shard_map/all_to_all | solution.py:290
  49.9 2.1 %collective-permute-start.8 = (bf16[128,1024]{1,0:T(8,128)(2,1)S(1)}, bf16[128,1024]{1,0:T(8,128)(2,1)S(1)}, u32[]{:S(2)}, u32[]{:S(2)}) collective-permute-start(bf16[128,1024]{1,0:T(8,128)(2,1)S(1)} %get-tuple-element.34.refs_0_), channel_id=1, source_target_pairs={{8,0},{16,8},{24,16},{32,24},{40,32},{48,40},{56,48},{64,56},{72,6... | collective-permute-start | bytes 786440 | tf_op jit(solution)/shard_map/ppermute | solution.py:32
  52.0 0.7 collective-permute-start.1
  52.6 0.7 collective-permute-start.2
  53.3 0.7 collective-permute-start.3
  54.0 0.7 collective-permute-start.4
  54.7 0.7 collective-permute-start.5
  55.4 26.3 %collective-permute-start.6 = (bf16[8,1152]{1,0:T(8,128)(2,1)S(1)}, bf16[8,1152]{1,0:T(8,128)(2,1)S(1)}, u32[]{:S(2)}, u32[]{:S(2)}) collective-permute-start(bf16[8,1152]{1,0:T(8,128)(2,1)S(1)} %reduce_sum.12), channel_id=1, source_target_pairs={{128,0},{129,1},{130,2},{131,3},{132,4},{133,5},{134,6},{135,7},{1... | collective-permute-start | bytes 55304 | tf_op jit(solution)/shard_map/ppermute | solution.py:45
  82.5 0.7 collective-permute-done.6
  83.2 0.7 collective-permute-start.10
  83.9 1.3 %collective-permute-start.9 = (bf16[8,1152]{1,0:T(8,128)(2,1)S(1)}, bf16[8,1152]{1,0:T(8,128)(2,1)S(1)}, u32[]{:S(2)}, u32[]{:S(2)}) collective-permute-start(bf16[8,1152]{1,0:T(8,128)(2,1)S(1)} %fusion), channel_id=1, source_target_pairs={{0,128},{1,129},{2,130},{3,131},{4,132},{5,133},{6,134},{7,135},{8... | collective-permute-start | bytes 55304 | tf_op jit(solution)/shard_map/ppermute | solution.py:54
  85.2 12.0 %collective-permute-done.9 = bf16[8,1152]{1,0:T(8,128)(2,1)S(1)} collective-permute-done((bf16[8,1152]{1,0:T(8,128)(2,1)S(1)}, bf16[8,1152]{1,0:T(8,128)(2,1)S(1)}, u32[]{:S(2)}, u32[]{:S(2)}) %collective-permute-start.9) | collective-permute-done | bytes 18464 | tf_op jit(solution)/shard_map/ppermute | solution.py:54
  97.2 1.3 %collective-permute-start.11 = (bf16[8,1152]{1,0:T(8,128)(2,1)S(1)}, bf16[8,1152]{1,0:T(8,128)(2,1)S(1)}, u32[]{:S(2)}, u32[]{:S(2)}) collective-permute-start(bf16[8,1152]{1,0:T(8,128)(2,1)S(1)} %add_add_fusion.1), channel_id=1, source_target_pairs={{896,512},{128,256},{897,513},{129,257},{898,514},{130,258},{899,5... | collective-permute-start | bytes 55304 | tf_op jit(solution)/shard_map/ppermute | solution.py:54
  99.2 0.8 collective-permute-done.11
  100.6 5.4 %shard_map.105 = (bf16[128,1024]{1,0:T(8,128)(2,1)}, bf16[128,1024]{1,0:T(8,128)(2,1)}) custom-call(s32[1]{0:T(128)} %bitcast.2.early, bf16[128,1024]{1,0:T(8,128)(2,1)S(1)} %get-tuple-element.35.early_k, bf16[128,1024]{1,0:T(8,128)(2,1)S(1)} %get-tuple-element.44.early_v, bf16[128,1024]{1,0:T(8,128)(2,1)S(1)} %get-tuple-element.34.refs_0_, ...), custom_call_target="tpu_custom_call" | custom-call | flops 33554432 | bytes 2621444 | tf_op jit(solution)/shard_map/pallas_call | solution.py:65
  106.1 16.1 %all_to_all.17 = bf16[16,8,1152]{2,1,0:T(8,128)(2,1)S(1)} all-to-all(bf16[16,8,1152]{2,1,0:T(8,128)(2,1)S(1)} %broadcast_in_dim.10), channel_id=1, replica_groups=mesh['zh'=8,'zl'=4,'x'=4,'tp'=8] {'zl','x'}, dimensions={0} | all-to-all | bytes 589824 | tf_op jit(solution)/shard_map/all_to_all | solution.py:38
  122.3 0.8 shard_map.106
  (32 shorter events, 2.2 us)
Async XLA Ops:
  0.6 4.7 %copy-start = (f32[128,1024]{1,0:T(8,128)S(1)}, f32[128,1024]{1,0:T(8,128)}, u32[]{:S(2)}) copy-start(f32[128,1024]{1,0:T(8,128)} %refs_2_.3) | copy-start | bytes 1572868
  1.8 13.4 %copy-start.3 = (bf16[128,1024]{1,0:T(8,128)(2,1)S(1)}, bf16[128,1024]{1,0:T(8,128)(2,1)}, u32[]{:S(2)}) copy-start(bf16[128,1024]{1,0:T(8,128)(2,1)} %query.3) | copy-start | bytes 786436
  1.8 13.4 %copy-start.4 = (bf16[128,1024]{1,0:T(8,128)(2,1)S(1)}, bf16[128,1024]{1,0:T(8,128)(2,1)}, u32[]{:S(2)}) copy-start(bf16[128,1024]{1,0:T(8,128)(2,1)} %cot.3) | copy-start | bytes 786436
  1.8 13.4 %collective-permute-start = (bf16[128,1024]{1,0:T(8,128)(2,1)S(1)}, bf16[128,1024]{1,0:T(8,128)(2,1)S(1)}, u32[]{:S(2)}, u32[]{:S(2)}) collective-permute-start(bf16[128,1024]{1,0:T(8,128)(2,1)S(1)} %multiply_convert_fusion.mixed), channel_id=1, source_target_pairs={{0,8},{8,16},{16,24},{24,32},{32,40},{40,48},{48,56},{56,64},{64,7... | collective-permute-start | bytes 786440 | tf_op jit(solution)/shard_map/ppermute | solution.py:32
  5.4 9.8 %copy-start.5 = (f32[1024]{0:T(1024)S(1)}, f32[1024]{0:T(1024)}, u32[]{:S(2)}) copy-start(f32[1024]{0:T(1024)} %param.11) | copy-start | bytes 12292
  33.4 49.0 %copy-start.2 = (bf16[128,1024]{1,0:T(8,128)(2,1)S(1)}, bf16[128,1024]{1,0:T(8,128)(2,1)}, u32[]{:S(2)}) copy-start(bf16[128,1024]{1,0:T(8,128)(2,1)} %refs_3_.3) | copy-start | bytes 786436
  49.9 32.5 %copy-start.1 = (bf16[128,1024]{1,0:T(8,128)(2,1)S(1)}, bf16[128,1024]{1,0:T(8,128)(2,1)}, u32[]{:S(2)}) copy-start(bf16[128,1024]{1,0:T(8,128)(2,1)} %refs_4_.3) | copy-start | bytes 786436
  49.9 31.8 %collective-permute-start.8 = (bf16[128,1024]{1,0:T(8,128)(2,1)S(1)}, bf16[128,1024]{1,0:T(8,128)(2,1)S(1)}, u32[]{:S(2)}, u32[]{:S(2)}) collective-permute-start(bf16[128,1024]{1,0:T(8,128)(2,1)S(1)} %get-tuple-element.34.refs_0_), channel_id=1, source_target_pairs={{8,0},{16,8},{24,16},{32,24},{40,32},{48,40},{56,48},{64,56},{72,6... | collective-permute-start | bytes 786440 | tf_op jit(solution)/shard_map/ppermute | solution.py:32
  52.0 2.7 %collective-permute-start.1 = (bf16[8,1152]{1,0:T(8,128)(2,1)S(1)}, bf16[8,1152]{1,0:T(8,128)(2,1)S(1)}, u32[]{:S(2)}, u32[]{:S(2)}) collective-permute-start(bf16[8,1152]{1,0:T(8,128)(2,1)S(1)} %reduce_sum.12), channel_id=1, source_target_pairs={{512,0},{513,1},{514,2},{515,3},{516,4},{517,5},{518,6},{519,7},{5... | collective-permute-start | bytes 55304 | tf_op jit(solution)/shard_map/ppermute | solution.py:45
  52.6 2.7 %collective-permute-start.2 = (bf16[8,1152]{1,0:T(8,128)(2,1)S(1)}, bf16[8,1152]{1,0:T(8,128)(2,1)S(1)}, u32[]{:S(2)}, u32[]{:S(2)}) collective-permute-start(bf16[8,1152]{1,0:T(8,128)(2,1)S(1)} %reduce_sum.12), channel_id=1, source_target_pairs={{640,0},{641,1},{642,2},{643,3},{644,4},{645,5},{646,6},{647,7},{6... | collective-permute-start | bytes 55304 | tf_op jit(solution)/shard_map/ppermute | solution.py:45
  53.3 29.1 %collective-permute-start.3 = (bf16[8,1152]{1,0:T(8,128)(2,1)S(1)}, bf16[8,1152]{1,0:T(8,128)(2,1)S(1)}, u32[]{:S(2)}, u32[]{:S(2)}) collective-permute-start(bf16[8,1152]{1,0:T(8,128)(2,1)S(1)} %reduce_sum.12), channel_id=1, source_target_pairs={{384,0},{385,1},{386,2},{387,3},{388,4},{389,5},{390,6},{391,7},{3... | collective-permute-start | bytes 55304 | tf_op jit(solution)/shard_map/ppermute | solution.py:45
  54.0 28.5 %collective-permute-start.4 = (bf16[8,1152]{1,0:T(8,128)(2,1)S(1)}, bf16[8,1152]{1,0:T(8,128)(2,1)S(1)}, u32[]{:S(2)}, u32[]{:S(2)}) collective-permute-start(bf16[8,1152]{1,0:T(8,128)(2,1)S(1)} %reduce_sum.12), channel_id=1, source_target_pairs={{256,0},{257,1},{258,2},{259,3},{260,4},{261,5},{262,6},{263,7},{2... | collective-permute-start | bytes 55304 | tf_op jit(solution)/shard_map/ppermute | solution.py:45
  54.7 27.8 %collective-permute-start.5 = (bf16[8,1152]{1,0:T(8,128)(2,1)S(1)}, bf16[8,1152]{1,0:T(8,128)(2,1)S(1)}, u32[]{:S(2)}, u32[]{:S(2)}) collective-permute-start(bf16[8,1152]{1,0:T(8,128)(2,1)S(1)} %reduce_sum.12), channel_id=1, source_target_pairs={{768,0},{769,1},{770,2},{771,3},{772,4},{773,5},{774,6},{775,7},{7... | collective-permute-start | bytes 55304 | tf_op jit(solution)/shard_map/ppermute | solution.py:45
  55.4 27.8 %collective-permute-start.6 = (bf16[8,1152]{1,0:T(8,128)(2,1)S(1)}, bf16[8,1152]{1,0:T(8,128)(2,1)S(1)}, u32[]{:S(2)}, u32[]{:S(2)}) collective-permute-start(bf16[8,1152]{1,0:T(8,128)(2,1)S(1)} %reduce_sum.12), channel_id=1, source_target_pairs={{128,0},{129,1},{130,2},{131,3},{132,4},{133,5},{134,6},{135,7},{1... | collective-permute-start | bytes 55304 | tf_op jit(solution)/shard_map/ppermute | solution.py:45
  81.7 1.4 %collective-permute-start.7 = (bf16[8,1152]{1,0:T(8,128)(2,1)S(1)}, bf16[8,1152]{1,0:T(8,128)(2,1)S(1)}, u32[]{:S(2)}, u32[]{:S(2)}) collective-permute-start(bf16[8,1152]{1,0:T(8,128)(2,1)S(1)} %reduce_sum.12), channel_id=1, source_target_pairs={{896,0},{897,1},{898,2},{899,3},{900,4},{901,5},{902,6},{903,7},{9... | collective-permute-start | bytes 55304 | tf_op jit(solution)/shard_map/ppermute | solution.py:45
  83.2 2.0 %collective-permute-start.10 = (bf16[8,1152]{1,0:T(8,128)(2,1)S(1)}, bf16[8,1152]{1,0:T(8,128)(2,1)S(1)}, u32[]{:S(2)}, u32[]{:S(2)}) collective-permute-start(bf16[8,1152]{1,0:T(8,128)(2,1)S(1)} %fusion), channel_id=1, source_target_pairs={{0,896},{1,897},{2,898},{3,899},{4,900},{5,901},{6,902},{7,903},{8... | collective-permute-start | bytes 55304 | tf_op jit(solution)/shard_map/ppermute | solution.py:54
  83.9 13.3 %collective-permute-start.9 = (bf16[8,1152]{1,0:T(8,128)(2,1)S(1)}, bf16[8,1152]{1,0:T(8,128)(2,1)S(1)}, u32[]{:S(2)}, u32[]{:S(2)}) collective-permute-start(bf16[8,1152]{1,0:T(8,128)(2,1)S(1)} %fusion), channel_id=1, source_target_pairs={{0,128},{1,129},{2,130},{3,131},{4,132},{5,133},{6,134},{7,135},{8... | collective-permute-start | bytes 55304 | tf_op jit(solution)/shard_map/ppermute | solution.py:54
  97.2 2.7 %collective-permute-start.11 = (bf16[8,1152]{1,0:T(8,128)(2,1)S(1)}, bf16[8,1152]{1,0:T(8,128)(2,1)S(1)}, u32[]{:S(2)}, u32[]{:S(2)}) collective-permute-start(bf16[8,1152]{1,0:T(8,128)(2,1)S(1)} %add_add_fusion.1), channel_id=1, source_target_pairs={{896,512},{128,256},{897,513},{129,257},{898,514},{130,258},{899,5... | collective-permute-start | bytes 55304 | tf_op jit(solution)/shard_map/ppermute | solution.py:54
  98.5 1.4 %collective-permute-start.12 = (bf16[8,1152]{1,0:T(8,128)(2,1)S(1)}, bf16[8,1152]{1,0:T(8,128)(2,1)S(1)}, u32[]{:S(2)}, u32[]{:S(2)}) collective-permute-start(bf16[8,1152]{1,0:T(8,128)(2,1)S(1)} %add_add_fusion.1), channel_id=1, source_target_pairs={{896,640},{897,641},{898,642},{899,643},{900,644},{901,645},{902,6... | collective-permute-start | bytes 55304 | tf_op jit(solution)/shard_map/ppermute | solution.py:54
  100.0 6.1 %collective-permute-start.13 = (bf16[8,1152]{1,0:T(8,128)(2,1)S(1)}, bf16[8,1152]{1,0:T(8,128)(2,1)S(1)}, u32[]{:S(2)}, u32[]{:S(2)}) collective-permute-start(bf16[8,1152]{1,0:T(8,128)(2,1)S(1)} %add_add_fusion), channel_id=1, source_target_pairs={{896,768},{256,384},{897,769},{257,385},{898,770},{258,386},{899,7... | collective-permute-start | bytes 55304 | tf_op jit(solution)/shard_map/ppermute | solution.py:54

commit v2 on v1

--- a/solution.py
+++ b/solution.py
@@ -12,10 +12,10 @@
 INWARDS = (4, 5, 3, 2, 6, 1, 7)
 OUTWARDS = (
     (((0, 1),), ((0, 7),)),
-    (((7, 4), (1, 2)), ((7, 5),)),
-    (((7, 6), (2, 3)),),
+    (((7, 4), (1, 2)), ((7, 5),), ((7, 6),)),
+    (((2, 3),),),
 )
-EARLY = 1
+EARLY = 2
 LANES = 128
 SUB = 8
 VMEM_BYTES = 8 << 20

time: 124 us -> 123 us (level)
  the two profiles are of different devices: /device:TPU:128 before, /device:TPU:256 now
where the time goes in v2:
time: 123 us
  waiting for transfers between devices  45.1 us (37%)
  blocking collectives  42.4 us (34%)
  Pallas kernels  17.1 us (14%)
  starting transfers between devices  16.1 us (13%)
  other arithmetic  1.26 us (1%)
    ppermute x6, waiting for transfers between devices, total(): moved.append(lax.ppermute(whole, FAR, pairs))  35.7 us
    pallas_call x6, Pallas kernels, call(): pl.pallas_call(kernel, out_shape=outs, in_specs=[in_smem if x.dtype == jn...  17.1 us
    all_to_all x1, blocking collectives, device_part(): block = lax.all_to_all(block, NEAR, 0, 0)  16.5 us
    all_to_all x1, blocking collectives, shared(): return lax.all_to_all(copies, axes, 0, 0)  16.1 us
    all_to_all x1, blocking collectives, device_part(): sums = lax.all_to_all(sums, 'tp', 0, 0)  9.72 us
    ppermute x2, waiting for transfers between devices, passed_along(): return lax.ppermute(value, CTX, pairs)  9.38 us
    ppermute x2, starting transfers between devices, passed_along(): return lax.ppermute(value, CTX, pairs)  5.58 us
    ppermute x7, starting transfers between devices, far_sum(): parts.append(lax.ppermute(value, FAR, [(cube, 0)]))  5.26 us
  transfers between devices with their start and end apart: 15, of which 3 were waited for; matrix products, arithmetic and copies ran while one was open for 0% of the time, Pallas kernels for 6%

profile of v2, /device:TPU:256, one launch (start us, length us, event | category | flops | bytes accessed | tf_op | source)
XLA Modules:
  0.0 122.9 jit_solution(8933188405952985572)
XLA Ops:
  0.6 1.2 multiply_convert_fusion.mixed
  1.8 3.5 %collective-permute-start = (bf16[128,1024]{1,0:T(8,128)(2,1)S(1)}, bf16[128,1024]{1,0:T(8,128)(2,1)S(1)}, u32[]{:S(2)}, u32[]{:S(2)}) collective-permute-start(bf16[128,1024]{1,0:T(8,128)(2,1)S(1)} %multiply_convert_fusion.mixed), channel_id=1, source_target_pairs={{0,8},{8,16},{16,24},{24,32},{32,40},{40,48},{48,56},{56,64},{64,7... | collective-permute-start | bytes 786440 | tf_op jit(solution)/shard_map/ppermute | solution.py:32
  5.4 2.4 %shard_map.101.own = f32[128,1024]{1,0:T(8,128)S(1)} custom-call(bf16[128,1024]{1,0:T(8,128)(2,1)S(1)} %multiply_convert_fusion.mixed, f32[128,1024]{1,0:T(8,128)S(1)} %copy-done), custom_call_target="tpu_custom_call" | custom-call | flops 16777216 | bytes 1310720 | tf_op jit(solution)/shard_map/pallas_call | solution.py:65
  7.8 7.4 %collective-permute-done.earlier = bf16[128,1024]{1,0:T(8,128)(2,1)S(1)} collective-permute-done((bf16[128,1024]{1,0:T(8,128)(2,1)S(1)}, bf16[128,1024]{1,0:T(8,128)(2,1)S(1)}, u32[]{:S(2)}, u32[]{:S(2)}) %collective-permute-start) | collective-permute-done | bytes 262176 | tf_op jit(solution)/shard_map/ppermute | solution.py:32
  15.2 2.8 %shard_map.102 = (f32[128,1024]{1,0:T(8,128)S(1)}, f32[8,8,128]{2,1,0:T(8,128)S(1)}) custom-call(f32[128,1024]{1,0:T(8,128)S(1)} %shard_map.101.own, bf16[128,1024]{1,0:T(8,128)(2,1)S(1)} %collective-permute-done.earlier, f32[128,1024]{1,0:T(8,128)S(1)} %copy-done, bf16[128,1024]{1,0:T(8,128)(2,1)S(1)} %copy-done.3, bf16[128,1024]{1,0:T(8,128)(2,1)S(1)} %copy-done.4, ...), custom_call_target="tpu_custom_call" | custom-call | flops 16777216 | bytes 2396160 | tf_op jit(solution)/shard_map/pallas_call | solution.py:65
  18.0 9.7 %all_to_all.15.sums = f32[8,8,128]{2,1,0:T(8,128)S(1)} all-to-all(f32[8,8,128]{2,1,0:T(8,128)S(1)} %get-tuple-element.28), channel_id=1, replica_groups=mesh['zh'=8,'zl'=4,'x'=4,'tp'=8] {'tp'}, dimensions={0} | all-to-all | bytes 65536 | tf_op jit(solution)/shard_map/all_to_all | solution.py:274
  27.7 5.7 %shard_map.103 = (bf16[128,1024]{1,0:T(8,128)(2,1)S(1)}, bf16[128,1024]{1,0:T(8,128)(2,1)}, bf16[128,1152]{1,0:T(8,128)(2,1)S(1)}) custom-call(f32[8,8,128]{2,1,0:T(8,128)S(1)} %all_to_all.15.sums, f32[128,1024]{1,0:T(8,128)S(1)} %get-tuple-element.29.conv, bf16[128,1024]{1,0:T(8,128)(2,1)S(1)} %copy-done.3, bf16[128,1024]{1,0:T(8,128)(2,1)S(1)} %copy-done.4, ...), custom_call_target="tpu_custom_call" | custom-call | flops 33554432 | bytes 2428928 | tf_op jit(solution)/shard_map/pallas_call | solution.py:65
  33.4 16.5 %all_to_all.16 = bf16[16,8,1152]{2,1,0:T(8,128)(2,1)S(1)} all-to-all(bf16[16,8,1152]{2,1,0:T(8,128)(2,1)S(1)} %bitcast.6), channel_id=1, replica_groups=mesh['zh'=8,'zl'=4,'x'=4,'tp'=8] {'zl','x'}, dimensions={0} | all-to-all | bytes 589824 | tf_op jit(solution)/shard_map/all_to_all | solution.py:290
  49.9 2.1 %collective-permute-start.8 = (bf16[128,1024]{1,0:T(8,128)(2,1)S(1)}, bf16[128,1024]{1,0:T(8,128)(2,1)S(1)}, u32[]{:S(2)}, u32[]{:S(2)}) collective-permute-start(bf16[128,1024]{1,0:T(8,128)(2,1)S(1)} %get-tuple-element.34.refs_0_), channel_id=1, source_target_pairs={{8,0},{16,8},{24,16},{32,24},{40,32},{48,40},{56,48},{64,56},{72,6... | collective-permute-start | bytes 786440 | tf_op jit(solution)/shard_map/ppermute | solution.py:32
  52.6 0.7 collective-permute-start.2
  53.3 0.7 collective-permute-start.3
  54.0 1.3 %collective-permute-start.4 = (bf16[8,1152]{1,0:T(8,128)(2,1)S(1)}, bf16[8,1152]{1,0:T(8,128)(2,1)S(1)}, u32[]{:S(2)}, u32[]{:S(2)}) collective-permute-start(bf16[8,1152]{1,0:T(8,128)(2,1)S(1)} %reduce_sum.12), channel_id=1, source_target_pairs={{256,0},{257,1},{258,2},{259,3},{260,4},{261,5},{262,6},{263,7},{2... | collective-permute-start | bytes 55304 | tf_op jit(solution)/shard_map/ppermute | solution.py:45
  55.3 0.7 collective-permute-start.5
  56.7 1.9 %collective-permute-done.8.refs_1_ = bf16[128,1024]{1,0:T(8,128)(2,1)S(1)} collective-permute-done((bf16[128,1024]{1,0:T(8,128)(2,1)S(1)}, bf16[128,1024]{1,0:T(8,128)(2,1)S(1)}, u32[]{:S(2)}, u32[]{:S(2)}) %collective-permute-start.8) | collective-permute-done | bytes 262176 | tf_op jit(solution)/shard_map/ppermute | solution.py:32
  59.4 0.7 collective-permute-start.10
  60.1 0.7 collective-permute-start.9
  60.8 1.3 %collective-permute-start.11 = (bf16[8,1152]{1,0:T(8,128)(2,1)S(1)}, bf16[8,1152]{1,0:T(8,128)(2,1)S(1)}, u32[]{:S(2)}, u32[]{:S(2)}) collective-permute-start(bf16[8,1152]{1,0:T(8,128)(2,1)S(1)} %add_add_fusion.1), channel_id=1, source_target_pairs={{896,512},{128,256},{897,513},{129,257},{898,514},{130,258},{899,5... | collective-permute-start | bytes 55304 | tf_op jit(solution)/shard_map/ppermute | solution.py:54
  62.1 0.7 collective-permute-start.12
  62.7 0.7 collective-permute-start.13
  63.4 35.7 %collective-permute-done.11 = bf16[8,1152]{1,0:T(8,128)(2,1)S(1)} collective-permute-done((bf16[8,1152]{1,0:T(8,128)(2,1)S(1)}, bf16[8,1152]{1,0:T(8,128)(2,1)S(1)}, u32[]{:S(2)}, u32[]{:S(2)}) %collective-permute-start.11) | collective-permute-done | bytes 18464 | tf_op jit(solution)/shard_map/ppermute | solution.py:54
  99.2 1.3 %collective-permute-start.14 = (bf16[8,1152]{1,0:T(8,128)(2,1)S(1)}, bf16[8,1152]{1,0:T(8,128)(2,1)S(1)}, u32[]{:S(2)}, u32[]{:S(2)}) collective-permute-start(bf16[8,1152]{1,0:T(8,128)(2,1)S(1)} %add_add_fusion), channel_id=1, source_target_pairs={{256,384},{257,385},{258,386},{259,387},{260,388},{261,389},{262,3... | collective-permute-start | bytes 55304 | tf_op jit(solution)/shard_map/ppermute | solution.py:54
  100.5 5.4 %shard_map.105 = (bf16[128,1024]{1,0:T(8,128)(2,1)}, bf16[128,1024]{1,0:T(8,128)(2,1)}) custom-call(s32[1]{0:T(128)} %bitcast.2.early, bf16[128,1024]{1,0:T(8,128)(2,1)S(1)} %get-tuple-element.35.early_k, bf16[128,1024]{1,0:T(8,128)(2,1)S(1)} %get-tuple-element.44.early_v, bf16[128,1024]{1,0:T(8,128)(2,1)S(1)} %get-tuple-element.34.refs_0_, ...), custom_call_target="tpu_custom_call" | custom-call | flops 33554432 | bytes 2621444 | tf_op jit(solution)/shard_map/pallas_call | solution.py:65
  105.9 16.1 %all_to_all.17 = bf16[16,8,1152]{2,1,0:T(8,128)(2,1)S(1)} all-to-all(bf16[16,8,1152]{2,1,0:T(8,128)(2,1)S(1)} %broadcast_in_dim.10), channel_id=1, replica_groups=mesh['zh'=8,'zl'=4,'x'=4,'tp'=8] {'zl','x'}, dimensions={0} | all-to-all | bytes 589824 | tf_op jit(solution)/shard_map/all_to_all | solution.py:38
  122.1 0.8 shard_map.106
  (34 shorter events, 2.2 us)
Async XLA Ops:
  0.6 4.7 %copy-start = (f32[128,1024]{1,0:T(8,128)S(1)}, f32[128,1024]{1,0:T(8,128)}, u32[]{:S(2)}) copy-start(f32[128,1024]{1,0:T(8,128)} %refs_2_.3) | copy-start | bytes 1572868
  1.8 13.4 %copy-start.3 = (bf16[128,1024]{1,0:T(8,128)(2,1)S(1)}, bf16[128,1024]{1,0:T(8,128)(2,1)}, u32[]{:S(2)}) copy-start(bf16[128,1024]{1,0:T(8,128)(2,1)} %query.3) | copy-start | bytes 786436
  1.8 13.4 %copy-start.4 = (bf16[128,1024]{1,0:T(8,128)(2,1)S(1)}, bf16[128,1024]{1,0:T(8,128)(2,1)}, u32[]{:S(2)}) copy-start(bf16[128,1024]{1,0:T(8,128)(2,1)} %cot.3) | copy-start | bytes 786436
  1.8 13.4 %collective-permute-start = (bf16[128,1024]{1,0:T(8,128)(2,1)S(1)}, bf16[128,1024]{1,0:T(8,128)(2,1)S(1)}, u32[]{:S(2)}, u32[]{:S(2)}) collective-permute-start(bf16[128,1024]{1,0:T(8,128)(2,1)S(1)} %multiply_convert_fusion.mixed), channel_id=1, source_target_pairs={{0,8},{8,16},{16,24},{24,32},{32,40},{40,48},{48,56},{56,64},{64,7... | collective-permute-start | bytes 786440 | tf_op jit(solution)/shard_map/ppermute | solution.py:32
  5.4 9.8 %copy-start.5 = (f32[1024]{0:T(1024)S(1)}, f32[1024]{0:T(1024)}, u32[]{:S(2)}) copy-start(f32[1024]{0:T(1024)} %param.11) | copy-start | bytes 12292
  33.4 25.9 %copy-start.2 = (bf16[128,1024]{1,0:T(8,128)(2,1)S(1)}, bf16[128,1024]{1,0:T(8,128)(2,1)}, u32[]{:S(2)}) copy-start(bf16[128,1024]{1,0:T(8,128)(2,1)} %refs_3_.3) | copy-start | bytes 786436
  49.9 9.4 %copy-start.1 = (bf16[128,1024]{1,0:T(8,128)(2,1)S(1)}, bf16[128,1024]{1,0:T(8,128)(2,1)}, u32[]{:S(2)}) copy-start(bf16[128,1024]{1,0:T(8,128)(2,1)} %refs_4_.3) | copy-start | bytes 786436
  49.9 8.7 %collective-permute-start.8 = (bf16[128,1024]{1,0:T(8,128)(2,1)S(1)}, bf16[128,1024]{1,0:T(8,128)(2,1)S(1)}, u32[]{:S(2)}, u32[]{:S(2)}) collective-permute-start(bf16[128,1024]{1,0:T(8,128)(2,1)S(1)} %get-tuple-element.34.refs_0_), channel_id=1, source_target_pairs={{8,0},{16,8},{24,16},{32,24},{40,32},{48,40},{56,48},{64,56},{72,6... | collective-permute-start | bytes 786440 | tf_op jit(solution)/shard_map/ppermute | solution.py:32
  52.0 3.3 %collective-permute-start.1 = (bf16[8,1152]{1,0:T(8,128)(2,1)S(1)}, bf16[8,1152]{1,0:T(8,128)(2,1)S(1)}, u32[]{:S(2)}, u32[]{:S(2)}) collective-permute-start(bf16[8,1152]{1,0:T(8,128)(2,1)S(1)} %reduce_sum.12), channel_id=1, source_target_pairs={{512,0},{513,1},{514,2},{515,3},{516,4},{517,5},{518,6},{519,7},{5... | collective-permute-start | bytes 55304 | tf_op jit(solution)/shard_map/ppermute | solution.py:45
  52.6 3.3 %collective-permute-start.2 = (bf16[8,1152]{1,0:T(8,128)(2,1)S(1)}, bf16[8,1152]{1,0:T(8,128)(2,1)S(1)}, u32[]{:S(2)}, u32[]{:S(2)}) collective-permute-start(bf16[8,1152]{1,0:T(8,128)(2,1)S(1)} %reduce_sum.12), channel_id=1, source_target_pairs={{640,0},{641,1},{642,2},{643,3},{644,4},{645,5},{646,6},{647,7},{6... | collective-permute-start | bytes 55304 | tf_op jit(solution)/shard_map/ppermute | solution.py:45
  53.3 6.0 %collective-permute-start.3 = (bf16[8,1152]{1,0:T(8,128)(2,1)S(1)}, bf16[8,1152]{1,0:T(8,128)(2,1)S(1)}, u32[]{:S(2)}, u32[]{:S(2)}) collective-permute-start(bf16[8,1152]{1,0:T(8,128)(2,1)S(1)} %reduce_sum.12), channel_id=1, source_target_pairs={{384,0},{385,1},{386,2},{387,3},{388,4},{389,5},{390,6},{391,7},{3... | collective-permute-start | bytes 55304 | tf_op jit(solution)/shard_map/ppermute | solution.py:45
  54.0 5.3 %collective-permute-start.4 = (bf16[8,1152]{1,0:T(8,128)(2,1)S(1)}, bf16[8,1152]{1,0:T(8,128)(2,1)S(1)}, u32[]{:S(2)}, u32[]{:S(2)}) collective-permute-start(bf16[8,1152]{1,0:T(8,128)(2,1)S(1)} %reduce_sum.12), channel_id=1, source_target_pairs={{256,0},{257,1},{258,2},{259,3},{260,4},{261,5},{262,6},{263,7},{2... | collective-permute-start | bytes 55304 | tf_op jit(solution)/shard_map/ppermute | solution.py:45
  55.3 4.0 %collective-permute-start.5 = (bf16[8,1152]{1,0:T(8,128)(2,1)S(1)}, bf16[8,1152]{1,0:T(8,128)(2,1)S(1)}, u32[]{:S(2)}, u32[]{:S(2)}) collective-permute-start(bf16[8,1152]{1,0:T(8,128)(2,1)S(1)} %reduce_sum.12), channel_id=1, source_target_pairs={{768,0},{769,1},{770,2},{771,3},{772,4},{773,5},{774,6},{775,7},{7... | collective-permute-start | bytes 55304 | tf_op jit(solution)/shard_map/ppermute | solution.py:45
  56.0 3.4 %collective-permute-start.6 = (bf16[8,1152]{1,0:T(8,128)(2,1)S(1)}, bf16[8,1152]{1,0:T(8,128)(2,1)S(1)}, u32[]{:S(2)}, u32[]{:S(2)}) collective-permute-start(bf16[8,1152]{1,0:T(8,128)(2,1)S(1)} %reduce_sum.12), channel_id=1, source_target_pairs={{128,0},{129,1},{130,2},{131,3},{132,4},{133,5},{134,6},{135,7},{1... | collective-permute-start | bytes 55304 | tf_op jit(solution)/shard_map/ppermute | solution.py:45
  58.6 0.8 collective-permute-start.7
  59.4 1.3 %collective-permute-start.10 = (bf16[8,1152]{1,0:T(8,128)(2,1)S(1)}, bf16[8,1152]{1,0:T(8,128)(2,1)S(1)}, u32[]{:S(2)}, u32[]{:S(2)}) collective-permute-start(bf16[8,1152]{1,0:T(8,128)(2,1)S(1)} %fusion), channel_id=1, source_target_pairs={{0,896},{1,897},{2,898},{3,899},{4,900},{5,901},{6,902},{7,903},{8... | collective-permute-start | bytes 55304 | tf_op jit(solution)/shard_map/ppermute | solution.py:54
  60.1 0.7 collective-permute-start.9
  60.8 38.4 %collective-permute-start.11 = (bf16[8,1152]{1,0:T(8,128)(2,1)S(1)}, bf16[8,1152]{1,0:T(8,128)(2,1)S(1)}, u32[]{:S(2)}, u32[]{:S(2)}) collective-permute-start(bf16[8,1152]{1,0:T(8,128)(2,1)S(1)} %add_add_fusion.1), channel_id=1, source_target_pairs={{896,512},{128,256},{897,513},{129,257},{898,514},{130,258},{899,5... | collective-permute-start | bytes 55304 | tf_op jit(solution)/shard_map/ppermute | solution.py:54
  62.1 37.1 %collective-permute-start.12 = (bf16[8,1152]{1,0:T(8,128)(2,1)S(1)}, bf16[8,1152]{1,0:T(8,128)(2,1)S(1)}, u32[]{:S(2)}, u32[]{:S(2)}) collective-permute-start(bf16[8,1152]{1,0:T(8,128)(2,1)S(1)} %add_add_fusion.1), channel_id=1, source_target_pairs={{896,640},{897,641},{898,642},{899,643},{900,644},{901,645},{902,6... | collective-permute-start | bytes 55304 | tf_op jit(solution)/shard_map/ppermute | solution.py:54
  62.7 36.4 %collective-permute-start.13 = (bf16[8,1152]{1,0:T(8,128)(2,1)S(1)}, bf16[8,1152]{1,0:T(8,128)(2,1)S(1)}, u32[]{:S(2)}, u32[]{:S(2)}) collective-permute-start(bf16[8,1152]{1,0:T(8,128)(2,1)S(1)} %add_add_fusion.1), channel_id=1, source_target_pairs={{896,768},{897,769},{898,770},{899,771},{900,772},{901,773},{902,7... | collective-permute-start | bytes 55304 | tf_op jit(solution)/shard_map/ppermute | solution.py:54
  99.2 6.7 %collective-permute-start.14 = (bf16[8,1152]{1,0:T(8,128)(2,1)S(1)}, bf16[8,1152]{1,0:T(8,128)(2,1)S(1)}, u32[]{:S(2)}, u32[]{:S(2)}) collective-permute-start(bf16[8,1152]{1,0:T(8,128)(2,1)S(1)} %add_add_fusion), channel_id=1, source_target_pairs={{256,384},{257,385},{258,386},{259,387},{260,388},{261,389},{262,3... | collective-permute-start | bytes 55304 | tf_op jit(solution)/shard_map/ppermute | solution.py:54
